TPU v7x, 128 devices: a whole 4x4x4 slice. The times are simulated.
128 devices in a mesh: dp: 2 (over core), seq: 4 (over x), tensor: 16 (over y, z).
Axes of the slice: x: 4, y: 4, z: 4, core: 2. Of those that a mesh axis runs over, the one named last changes fastest.
Arguments:
- tokens: bfloat16 [16384, 4096], P(('dp', 'seq', 'tensor')), may hold values from -6 to 6
- cotangent: bfloat16 [16384, 14336], P(('dp', 'seq', 'tensor')), may hold values from -0.046875 to 0.046875
- master: bfloat16 [8, 336, 128, 128], P(None, 'tensor'), as said below
- block_ids: int32 [8, 336], P(None, 'tensor'), may hold values from 0 to 223, as said below
- live_count: int32 [8, 16], P(None, 'tensor'), may hold values from 1 to 21, as said below
Outputs:
- outputs: bfloat16 [16384, 14336], P(('dp', 'seq', 'tensor'))
- w_grad: float32 [8, 336, 128, 128], P(('dp', 'seq'), 'tensor')
Inputs may be any that keep to these rules, and one draw needn't show every extreme that they name: Within each group t the 168 entries block_ids[:, t * 21 : (t + 1) * 21] are distinct. `live_count`: in every group one owner uses all 21 slots. `master`: in every block one entry has the largest magnitude, and no entry of a block, divided by that magnitude over 7, lies within 0.1 of a half-integer.
All inputs are finite; a program needn't handle non-finite values. Where the computation divides by a largest or mean magnitude, that divisor is 1e-20 or more.
Results may differ from a plain program's by a relative error of at most 0.005.
Values may be sent and summed in bfloat16 or wider, within the bound.
A program may use at most 192 MiB of HBM per device.

v0:
```python
import jax
import jax.numpy as jnp
from jax import lax
from jax.sharding import PartitionSpec as P

BS = 128


def fake_quant(master, live_mask):
    master_wide = master.astype(jnp.float32)
    block_peak = jnp.max(jnp.abs(master_wide), axis=(-2, -1), keepdims=True) + 1e-06
    levels = jnp.floor(master_wide * (7.0 / block_peak) + 0.5)
    return (levels * (block_peak / 7.0) * live_mask[..., None, None]).astype(jnp.bfloat16)


def assemble(quantized, slot_ids, row_blocks, col_blocks):
    total_slots = quantized.shape[0]
    block_numbers = jnp.arange(row_blocks * col_blocks, dtype=jnp.int32)
    slot_numbers = jnp.arange(1, total_slots + 1, dtype=jnp.int32)
    matches = (slot_ids[:, None] == block_numbers[None, :]).astype(jnp.int32)
    slot_of_block = jnp.sum(matches * slot_numbers[:, None], axis=0)
    padded = jnp.concatenate([jnp.zeros((1, BS, BS), jnp.bfloat16), quantized], axis=0)
    placed = jnp.take(padded, slot_of_block, axis=0).reshape(row_blocks, col_blocks, BS, BS)
    return placed.transpose(0, 2, 1, 3).reshape(row_blocks * BS, col_blocks * BS)


def dense_gradient(token_rows, grad_rows):
    return lax.dot_general(
        token_rows, grad_rows, (((0,), (0,)), ((), ())), preferred_element_type=jnp.float32
    )


def pick_blocks(full_grad, slot_ids, row_blocks, col_blocks):
    grid_blocks = full_grad.reshape(row_blocks, BS, col_blocks, BS).transpose(0, 2, 1, 3)
    grid_blocks = grid_blocks.reshape(row_blocks * col_blocks, BS, BS)
    return jnp.take(grid_blocks, slot_ids, axis=0)


def shards(tokens, cotangent, master, block_ids, live_count):
    owners, slots = block_ids.shape
    groups = lax.axis_size("tensor")
    live_mask = (jnp.arange(slots, dtype=jnp.int32)[None, :] < live_count).astype(jnp.float32)
    quantized = fake_quant(master, live_mask).reshape(owners * slots, BS, BS)
    slot_ids = block_ids.reshape(owners * slots)
    row_blocks = tokens.shape[1] // BS
    col_blocks = cotangent.shape[1] // (BS * groups)
    dense_weight = assemble(quantized, slot_ids, row_blocks, col_blocks)
    grads_local = lax.all_to_all(cotangent, "tensor", split_axis=1, concat_axis=0, tiled=True)
    gathered = lax.all_gather(tokens, "tensor", axis=0, tiled=True)
    results = jnp.dot(gathered, dense_weight, preferred_element_type=jnp.float32)
    full_grad = dense_gradient(gathered, grads_local)
    outputs = lax.all_to_all(
        results.astype(jnp.bfloat16), "tensor", split_axis=0, concat_axis=1, tiled=True
    )
    partial_value = pick_blocks(full_grad, slot_ids, row_blocks, col_blocks)
    partial_value = (partial_value * live_mask.reshape(owners * slots)[:, None, None]).reshape(
        owners, slots, BS, BS
    )
    w_grad = lax.psum_scatter(partial_value, ("dp", "seq"), scatter_dimension=0, tiled=True)
    return (outputs, w_grad)


def solution(mesh):
    return jax.shard_map(
        shards,
        mesh=mesh,
        in_specs=(
            P(("dp", "seq", "tensor"), None),
            P(("dp", "seq", "tensor"), None),
            P(None, "tensor", None, None),
            P(None, "tensor"),
            P(None, "tensor"),
        ),
        out_specs=(P(("dp", "seq", "tensor"), None), P(("dp", "seq"), "tensor", None, None)),
        check_vma=False,
    )
```

profile of v0, /device:TPU:1, one launch (start us, length us, event | category | flops | bytes accessed | tf_op | source)
XLA Modules:
  0.0 369.7 jit_solution(11243594162319001183)
XLA Ops:
  7.2 0.7 all-gather.2.cloned.1.call-update
  7.9 6.1 %copy.33 = bf16[128,14336]{0,1:T(8,128)(2,1)} copy(bf16[128,14336]{1,0:T(8,128)(2,1)} %param.6) | data formatting | bytes 7340032 | tf_op args[1]
  14.0 6.1 %copy.34 = bf16[128,16,896]{2,0,1:T(8,128)(2,1)} copy(bf16[128,16,896]{0,2,1:T(8,128)(2,1)} %bitcast.55) | data formatting | bytes 7340032 | tf_op jit(solution)/shard_map/all_to_all | solution.py:48
  20.1 8.6 %all-to-all-start.1 = ((bf16[128,16,896]{2,0,1:T(8,128)(2,1)}), bf16[128,16,896]{2,0,1:T(8,128)(2,1)}, u32[]{:S(2)}, u32[]{:S(2)}) async-start(bf16[128,16,896]{2,0,1:T(8,128)(2,1)} %copy.34), calls=%async_computation.1 | async-start | bytes 7340032 | tf_op jit(solution)/shard_map/all_to_all | solution.py:48
  28.8 0.1 reshape.139
  29.0 4.0 %fusion = f32[8,21]{1,0:T(8,128)S(1)} fusion(bf16[8,21,128,128]{3,2,1,0:T(8,128)(2,1)} %param.7), kind=kLoop, calls=%fused_computation.4 | loop fusion | flops 8257368 | bytes 5505696 | tf_op jit(solution)/shard_map/reduce_max | solution.py:11
  32.9 68.2 %all-to-all-done.1 = bf16[128,16,896]{2,0,1:T(8,128)(2,1)} async-done(((bf16[128,16,896]{2,0,1:T(8,128)(2,1)}), bf16[128,16,896]{2,0,1:T(8,128)(2,1)}, u32[]{:S(2)}, u32[]{:S(2)}) %all-to-all-start.1) | async-done | bytes 3670048 | tf_op jit(solution)/shard_map/all_to_all | solution.py:48
  101.2 6.1 %copy.35 = bf16[2048,896]{0,1:T(8,128)(2,1)} copy(bf16[2048,896]{1,0:T(8,128)(2,1)} %bitcast.15) | data formatting | bytes 7340032 | tf_op jit(solution)/shard_map/all_to_all | solution.py:48
  107.2 57.2 %all-gather.2.cloned.1.call-done = bf16[2048,4096]{1,0:T(8,128)(2,1)} async-done(((bf16[128,4096]{1,0:T(8,128)(2,1)}), bf16[2048,4096]{1,0:T(8,128)(2,1)}) %all-gather.2.cloned.1.call-update) | async-done | bytes 16777232 | tf_op jit(solution)/shard_map/all_gather | solution.py:49
  164.5 22.5 %copy.32 = bf16[4096,2048]{1,0:T(8,128)(2,1)} copy(bf16[4096,2048]{0,1:T(8,128)(2,1)} %bitcast.51) | data formatting | bytes 33554432 | tf_op jit(solution)/shard_map/dot_general | solution.py:28
  187.0 23.3 %fusion.12 = f32[32,128,7,128]{3,1,2,0:T(8,128)} fusion(bf16[32,128,2048,1]{2,1,3,0:T(8,128)(2,1)} %bitcast.52, bf16[7,128,2048,1]{2,1,0,3:T(8,128)(2,1)} %bitcast.58), kind=kOutput, calls=%fused_computation.32 | convolution fusion | flops 15032385536 | bytes 35127296 | tf_op jit(solution)/shard_map/dot_general | solution.py:28
  210.3 15.5 %gather_fusion.1 = f32[168,128,128]{2,1,0:T(8,128)} fusion(f32[224,128,128]{2,1,0:T(8,128)} %bitcast.56, s32[1024]{0:T(1024)S(1)} %pad_clamp_fusion), kind=kCustom, calls=%fused_computation.1 | custom fusion | bytes 22020768 | tf_op jit(solution)/shard_map/jit(_take)/gather | solution.py:36
  225.8 14.1 %select_multiply_fusion = (f32[8,21,128,128]{3,2,1,0:T(8,128)}, bf16[8,21,128,128]{3,2,1,0:T(8,128)(2,1)}) fusion(f32[8,21,128,128]{3,2,1,0:T(8,128)} %bitcast.48, f32[8,21]{1,0:T(8,128)S(1)} %get-tuple-element.12, pred[8,21]{1,0:T(8,128)(4,1)S(1)} %get-tuple-element.13, f32[8,21]{1,0:T(8,128)S(1)} %get-tuple-element.11, f32[8,21]{1,0:T(8,128)S(1)} %get-tuple-element.10, ...), kind=kLoop, calls=%fused_computation.10 | loop fusion | flops 24772608 | bytes 33032328 | tf_op jit(solution)/shard_map/mul | solution.py:56
  240.0 0.1 select_reduce_fusion
  240.2 0.1 reduce_sum.14
  240.3 7.2 %concatenate.3 = bf16[169,128,128]{2,1,0:T(8,128)(2,1)} pad(bf16[168,128,128]{2,1,0:T(8,128)(2,1)} %bitcast.50, bf16[]{:T(256)} %constant.42.clone.1), padding=1_0x0_0x0_0 | pad | bytes 11042818 | tf_op jit(solution)/shard_map/concatenate | solution.py:22
  247.5 11.1 %gather_fusion = bf16[224,128,128]{2,1,0:T(8,128)(2,1)} fusion(bf16[169,128,128]{2,1,0:T(8,128)(2,1)} %concatenate.3, s32[1024]{0:T(1024)S(1)} %pad_clamp_fusion.1), kind=kCustom, calls=%fused_computation | custom fusion | bytes 14680960 | tf_op jit(solution)/shard_map/jit(_take)/gather | solution.py:23
  258.6 6.8 %select_bitcast_fusion = bf16[32,128,7,128]{3,1,2,0:T(8,128)(2,1)} fusion(bf16[32,7,128,128]{3,2,1,0:T(8,128)(2,1)} %bitcast.49, pred[32,7]{1,0:T(8,128)(4,1)S(1)} %compare_and_fusion), kind=kLoop, calls=%fused_computation.14 | loop fusion | flops 3670016 | bytes 14680288 | tf_op jit(solution)/shard_map/transpose | solution.py:24
  265.4 12.2 %copy.30 = bf16[32,128,7,128]{1,0,3,2:T(8,128)(2,1)} copy(bf16[32,128,7,128]{3,1,2,0:T(8,128)(2,1)} %select_bitcast_fusion) | data formatting | bytes 14680064 | tf_op jit(solution)/shard_map/transpose | solution.py:24
  277.6 20.9 %convert_bitcast_fusion = bf16[112,16,8,128]{3,2,1,0:T(8,128)(2,1)S(1)} fusion(bf16[2048,4096]{1,0:T(8,128)(2,1)} %all-gather.2.cloned.1.call-done, bf16[112,8,32,128]{3,2,1,0:T(8,128)(2,1)} %bitcast.57), kind=kOutput, calls=%fused_computation.16 | convolution fusion | flops 15034220544 | bytes 27787264 | tf_op jit(solution)/shard_map/dot_general | solution.py:50
  298.5 0.9 copy.47
  299.5 55.9 %all_to_all.38 = bf16[16,128,896]{1,2,0:T(8,128)(2,1)} all-to-all(bf16[16,128,896]{1,2,0:T(8,128)(2,1)S(1)} %bitcast.53), channel_id=1, replica_groups=mesh['dp'=2,'seq'=4,'tensor'=16] {'tensor'}, dimensions={0} | all-to-all | bytes 7340032 | tf_op jit(solution)/shard_map/all_to_all | solution.py:52
  355.3 6.1 %copy.36 = bf16[128,14336]{1,0:T(8,128)(2,1)} copy(bf16[128,14336]{0,1:T(8,128)(2,1)} %bitcast.54) | data formatting | bytes 7340032
  361.5 1.4 reduce-scatter.2.cloned.1.call-done
  (16 shorter events, 0.3 us)
Async XLA Ops:
  7.2 157.3 %all-gather.2.cloned.1.call-start = ((), (), s32[]{:S(2)}) async-start(), calls=%async_computation.3 | async-start | bytes 17825792 | tf_op jit(solution)/shard_map/all_gather | solution.py:49
  13.9 14.8 %copy-start = (s32[8,21]{1,0:T(8,128)S(1)}, s32[8,21]{1,0:T(8,128)}, u32[]{:S(2)}) copy-start(s32[8,21]{1,0:T(8,128)} %param.8) | copy-start | bytes 2020
  13.9 14.9 %copy-start.1 = (s32[8,1]{0,1:T(1,128)S(1)}, s32[8,1]{0,1:T(1,128)}, u32[]{:S(2)}) copy-start(s32[8,1]{0,1:T(1,128)} %param.9) | copy-start | bytes 100
  20.1 81.1 %all-to-all-start.1 = ((bf16[128,16,896]{2,0,1:T(8,128)(2,1)}), bf16[128,16,896]{2,0,1:T(8,128)(2,1)}, u32[]{:S(2)}, u32[]{:S(2)}) async-start(bf16[128,16,896]{2,0,1:T(8,128)(2,1)} %copy.34), calls=%async_computation.1 | async-start | bytes 7340032 | tf_op jit(solution)/shard_map/all_to_all | solution.py:48
  28.7 334.1 %reduce-scatter.2.cloned.1.call-start = ((), (), s32[]{:S(2)}) async-start(), calls=%async_computation.4 | async-start | bytes 12386304 | tf_op jit(solution)/shard_map/reduce_scatter | solution.py:59
Sparse Core Ops, SparseCore 0:
  10.1 154.2 all-gather.1
  240.1 122.7 reduce-scatter.1
where the time goes:
time: 371 us; the launch traced here: 370 us
  waiting for transfers between devices  128 us (35%)
  local copies, waits for them, and re-layouts  94.1 us (25%)
  blocking collectives  55.9 us (15%)
  matrix products  44.2 us (12%)
  other arithmetic  25.1 us (7%)
  between operations  14.1 us (4%)
  starting transfers between devices  8.72 us (2%)
    all_to_all x1, waiting for transfers between devices, shards(): lax.all_to_all(cotangent, 'tensor', split_axis=1, concat_axis=0, tiled=True)  68.2 us
    all_gather x1, waiting for transfers between devices, shards(): gathered = lax.all_gather(tokens, 'tensor', axis=0, tiled=True)  57.2 us
    all_to_all x1, blocking collectives, shards(): lax.all_to_all(results.astype(jnp.bfloat16), 'tensor', split_axis=0, conc...  55.9 us
    dot_general x1, matrix products, dense_gradient(): lax.dot_general(token_rows, grad_rows, (((0,), (0,)), ((), ())), preferre...  23.3 us
    dot_general x1, local copies, waits for them, and re-layouts, dense_gradient(): lax.dot_general(token_rows, grad_rows, (((0,), (0,)), ((), ())), preferre...  22.5 us
    dot_general x1, matrix products, shards(): jnp.dot(gathered, dense_weight, preferred_element_type=jnp.float32)  20.9 us
    gather x1, local copies, waits for them, and re-layouts, pick_blocks(): return jnp.take(grid_blocks, slot_ids, axis=0)  15.5 us
    mul x1, other arithmetic, shards(): partial_value * live_mask.reshape(owners * slots)[:, None, None]  14.1 us
  transfers between devices with their start and end apart: 3, of which 3 were waited for; matrix products, arithmetic and copies ran while one was open for 24% of the time, Pallas kernels for 0%

commit v1 on v0

--- a/solution.py
+++ b/solution.py
@@ -46,7 +46,8 @@
     col_blocks = cotangent.shape[1] // (BS * groups)
     dense_weight = assemble(quantized, slot_ids, row_blocks, col_blocks)
     grads_local = lax.all_to_all(cotangent, "tensor", split_axis=1, concat_axis=0, tiled=True)
-    gathered = lax.all_gather(tokens, "tensor", axis=0, tiled=True)
+    sent = jnp.stack([tokens] * lax.axis_size("tensor"))
+    gathered = jnp.concatenate(lax.all_to_all(sent, "tensor", 0, 0), axis=0)
     results = jnp.dot(gathered, dense_weight, preferred_element_type=jnp.float32)
     full_grad = dense_gradient(gathered, grads_local)
     outputs = lax.all_to_all(

time: 371 us -> 623 us (1.68)
  waiting for transfers between devices: 128 us -> 346 us
  local copies, waits for them, and re-layouts: 94.1 us -> 122 us
  starting transfers between devices: 8.72 us -> 20.6 us
  blocking collectives: 55.9 us -> 47.8 us
    all_to_all x0 -> x1, waiting for transfers between devices: none -> 285 us  [shards(): gathered = jnp.concatenate(lax.all_to_all(sent, 'tensor', 0, 0), axis=0)]
    all_gather x1 -> x0, waiting for transfers between devices: 57.2 us -> none  [shards(): gathered = lax.all_gather(tokens, 'tensor', axis=0, tiled=True)]
    all_to_all x0 -> x1, local copies, waits for them, and re-layouts: none -> 21.4 us  [shards(): gathered = jnp.concatenate(lax.all_to_all(sent, 'tensor', 0, 0), axis=0)]
    all_to_all x1, waiting for transfers between devices: 68.2 us -> 48.5 us  [shards(): lax.all_to_all(cotangent, 'tensor', split_axis=1, concat_axis=0, tiled=True)]
    all_to_all x0 -> x1, starting transfers between devices: none -> 11.9 us  [shards(): gathered = jnp.concatenate(lax.all_to_all(sent, 'tensor', 0, 0), axis=0)]
    reduce_scatter x1, waiting for transfers between devices: 1.39 us -> 12.4 us  [shards(): lax.psum_scatter(partial_value, ('dp', 'seq'), scatter_dimension=0, tiled...]
    all_to_all x1, blocking collectives: 55.9 us -> 47.8 us  [shards(): lax.all_to_all(results.astype(jnp.bfloat16), 'tensor', split_axis=0, conc...]
    unnamed x6 -> x9, local copies, waits for them, and re-layouts: 12.2 us -> 12.8 us
  transfers between devices with their start and end apart: 3 -> 3, of which waited for: 3 -> 3; matrix products, arithmetic and copies ran while one was open for 24% -> 12% of each run, Pallas kernels for 0% -> 0%
where the time goes in v1:
time: 623 us; the launch traced here: 621 us
  waiting for transfers between devices  346 us (56%)
  local copies, waits for them, and re-layouts  122 us (20%)
  blocking collectives  47.8 us (8%)
  matrix products  44.2 us (7%)
  other arithmetic  25.6 us (4%)
  starting transfers between devices  20.6 us (3%)
  between operations  14.1 us (2%)
    all_to_all x1, waiting for transfers between devices, shards(): gathered = jnp.concatenate(lax.all_to_all(sent, 'tensor', 0, 0), axis=0)  285 us
    all_to_all x1, waiting for transfers between devices, shards(): lax.all_to_all(cotangent, 'tensor', split_axis=1, concat_axis=0, tiled=True)  48.5 us
    all_to_all x1, blocking collectives, shards(): lax.all_to_all(results.astype(jnp.bfloat16), 'tensor', split_axis=0, conc...  47.8 us
    dot_general x1, matrix products, dense_gradient(): lax.dot_general(token_rows, grad_rows, (((0,), (0,)), ((), ())), preferre...  23.3 us
    dot_general x1, local copies, waits for them, and re-layouts, dense_gradient(): lax.dot_general(token_rows, grad_rows, (((0,), (0,)), ((), ())), preferre...  22.5 us
    all_to_all x1, local copies, waits for them, and re-layouts, shards(): gathered = jnp.concatenate(lax.all_to_all(sent, 'tensor', 0, 0), axis=0)  21.4 us
    dot_general x1, matrix products, shards(): jnp.dot(gathered, dense_weight, preferred_element_type=jnp.float32)  20.9 us
    gather x1, local copies, waits for them, and re-layouts, pick_blocks(): return jnp.take(grid_blocks, slot_ids, axis=0)  15.5 us
  transfers between devices with their start and end apart: 3, of which 3 were waited for; matrix products, arithmetic and copies ran while one was open for 12% of the time, Pallas kernels for 0%

profile of v1, /device:TPU:1, one launch (start us, length us, event | category | flops | bytes accessed | tf_op | source)
XLA Modules:
  0.0 620.9 jit_solution(14415822602403579232)
XLA Ops:
  7.2 6.1 copy.37
  13.2 6.2 copy.38
  19.4 8.6 %all-to-all-start.2 = ((bf16[128,16,896]{2,0,1:T(8,128)(2,1)}), bf16[128,16,896]{2,0,1:T(8,128)(2,1)}, u32[]{:S(2)}, u32[]{:S(2)}) async-start(bf16[128,16,896]{2,0,1:T(8,128)(2,1)} %copy.38), calls=%async_computation.2 | async-start | bytes 7340032 | tf_op jit(solution)/shard_map/all_to_all | solution.py:48
  28.1 0.7 copy.33
  28.7 48.5 %all-to-all-done.2 = bf16[128,16,896]{2,0,1:T(8,128)(2,1)} async-done(((bf16[128,16,896]{2,0,1:T(8,128)(2,1)}), bf16[128,16,896]{2,0,1:T(8,128)(2,1)}, u32[]{:S(2)}, u32[]{:S(2)}) %all-to-all-start.2) | async-done | bytes 3670048 | tf_op jit(solution)/shard_map/all_to_all | solution.py:48
  77.3 6.1 stack.2
  83.3 11.9 %all-to-all-start = ((bf16[16,128,4096]{1,2,0:T(8,128)(2,1)}), bf16[16,128,4096]{1,2,0:T(8,128)(2,1)}, u32[]{:S(2)}, u32[]{:S(2)}) async-start(bf16[16,128,4096]{1,2,0:T(8,128)(2,1)} %stack.2), calls=%async_computation | async-start | bytes 33554432 | tf_op jit(solution)/shard_map/all_to_all | solution.py:50
  95.5 3.9 fusion
  99.4 6.1 copy.39
  105.4 285.3 %all-to-all-done = bf16[16,128,4096]{1,2,0:T(8,128)(2,1)} async-done(((bf16[16,128,4096]{1,2,0:T(8,128)(2,1)}), bf16[16,128,4096]{1,2,0:T(8,128)(2,1)}, u32[]{:S(2)}, u32[]{:S(2)}) %all-to-all-start) | async-done | bytes 16777248 | tf_op jit(solution)/shard_map/all_to_all | solution.py:50
  390.7 21.4 %copy.34 = bf16[16,128,4096]{2,1,0:T(8,128)(2,1)} copy(bf16[16,128,4096]{1,2,0:T(8,128)(2,1)} %all-to-all-done) | data formatting | bytes 33554432 | tf_op jit(solution)/shard_map/all_to_all | solution.py:50
  412.2 22.5 %copy.36 = bf16[4096,2048]{1,0:T(8,128)(2,1)} copy(bf16[4096,2048]{0,1:T(8,128)(2,1)} %bitcast.50) | data formatting | bytes 33554432 | tf_op jit(solution)/shard_map/dot_general | solution.py:28
  434.7 23.3 %fusion.12 = f32[32,128,7,128]{3,1,2,0:T(8,128)} fusion(bf16[32,128,2048,1]{2,1,3,0:T(8,128)(2,1)} %bitcast.55, bf16[7,128,2048,1]{2,1,0,3:T(8,128)(2,1)} %bitcast.61), kind=kOutput, calls=%fused_computation.32 | convolution fusion | flops 15032385536 | bytes 35127296 | tf_op jit(solution)/shard_map/dot_general | solution.py:28
  458.0 15.5 %gather_fusion.1 = f32[168,128,128]{2,1,0:T(8,128)} fusion(f32[224,128,128]{2,1,0:T(8,128)} %bitcast.59, s32[1024]{0:T(1024)S(1)} %pad_clamp_fusion), kind=kCustom, calls=%fused_computation.1 | custom fusion | bytes 22020768 | tf_op jit(solution)/shard_map/jit(_take)/gather | solution.py:36
  473.5 14.1 %select_multiply_fusion = (f32[8,21,128,128]{3,2,1,0:T(8,128)}, bf16[8,21,128,128]{3,2,1,0:T(8,128)(2,1)}) fusion(f32[8,21,128,128]{3,2,1,0:T(8,128)} %bitcast.52, f32[8,21]{1,0:T(8,128)S(1)} %get-tuple-element.12, pred[8,21]{1,0:T(8,128)(4,1)S(1)} %get-tuple-element.13, f32[8,21]{1,0:T(8,128)S(1)} %get-tuple-element.11, f32[8,21]{1,0:T(8,128)S(1)} %get-tuple-element.10, ...), kind=kLoop, calls=%fused_computation.10 | loop fusion | flops 24772608 | bytes 33032328 | tf_op jit(solution)/shard_map/mul | solution.py:57
  488.0 7.2 %concatenate.3 = bf16[169,128,128]{2,1,0:T(8,128)(2,1)} pad(bf16[168,128,128]{2,1,0:T(8,128)(2,1)} %bitcast.54, bf16[]{:T(256)} %constant.42.clone.1), padding=1_0x0_0x0_0 | pad | bytes 11042818 | tf_op jit(solution)/shard_map/concatenate | solution.py:22
  495.2 11.1 %gather_fusion = bf16[224,128,128]{2,1,0:T(8,128)(2,1)} fusion(bf16[169,128,128]{2,1,0:T(8,128)(2,1)} %concatenate.3, s32[1024]{0:T(1024)S(1)} %pad_clamp_fusion.1), kind=kCustom, calls=%fused_computation | custom fusion | bytes 14680960 | tf_op jit(solution)/shard_map/jit(_take)/gather | solution.py:23
  506.3 7.3 %select_bitcast_fusion = bf16[32,128,7,128]{3,1,2,0:T(8,128)(2,1)} fusion(bf16[32,7,128,128]{3,2,1,0:T(8,128)(2,1)} %bitcast.53, pred[32,7]{1,0:T(8,128)(4,1)S(1)} %compare_and_fusion), kind=kLoop, calls=%fused_computation.14 | loop fusion | flops 3670016 | bytes 14680288 | tf_op jit(solution)/shard_map/transpose | solution.py:24
  513.6 12.1 %copy.32 = bf16[32,128,7,128]{1,0,3,2:T(8,128)(2,1)} copy(bf16[32,128,7,128]{3,1,2,0:T(8,128)(2,1)} %select_bitcast_fusion) | data formatting | bytes 14680064 | tf_op jit(solution)/shard_map/transpose | solution.py:24
  525.8 20.9 %convert_bitcast_fusion = bf16[112,16,8,128]{3,2,1,0:T(8,128)(2,1)S(1)} fusion(bf16[2048,4096]{1,0:T(8,128)(2,1)} %bitcast.51, bf16[112,8,32,128]{3,2,1,0:T(8,128)(2,1)} %bitcast.60), kind=kOutput, calls=%fused_computation.16 | convolution fusion | flops 15034220544 | bytes 27787264 | tf_op jit(solution)/shard_map/dot_general | solution.py:51
  546.7 0.9 copy.51
  547.7 47.8 %all_to_all.43 = bf16[16,128,896]{1,2,0:T(8,128)(2,1)} all-to-all(bf16[16,128,896]{1,2,0:T(8,128)(2,1)S(1)} %bitcast.56), channel_id=1, replica_groups=mesh['dp'=2,'seq'=4,'tensor'=16] {'tensor'}, dimensions={0} | all-to-all | bytes 7340032 | tf_op jit(solution)/shard_map/all_to_all | solution.py:53
  595.5 6.1 copy.40
  601.6 12.4 %reduce-scatter.2.cloned.1.call-done = f32[1,21,128,128]{3,2,1,0:T(8,128)} async-done(((f32[8,21,128,128]{3,2,1,0:T(8,128)}), f32[1,21,128,128]{3,2,1,0:T(8,128)}) %reduce-scatter.2.cloned.1.call-update) | async-done | bytes 1376272 | tf_op jit(solution)/shard_map/reduce_scatter | solution.py:60
  (20 shorter events, 0.6 us)
Async XLA Ops:
  13.2 14.8 %copy-start = (bf16[128,4096]{1,0:T(8,128)(2,1)S(1)}, bf16[128,4096]{1,0:T(8,128)(2,1)}, u32[]{:S(2)}) copy-start(bf16[128,4096]{1,0:T(8,128)(2,1)} %param.5) | copy-start | bytes 3145732
  19.4 57.9 %all-to-all-start.2 = ((bf16[128,16,896]{2,0,1:T(8,128)(2,1)}), bf16[128,16,896]{2,0,1:T(8,128)(2,1)}, u32[]{:S(2)}, u32[]{:S(2)}) async-start(bf16[128,16,896]{2,0,1:T(8,128)(2,1)} %copy.38), calls=%async_computation.2 | async-start | bytes 7340032 | tf_op jit(solution)/shard_map/all_to_all | solution.py:48
  83.3 11.9 %copy-start.1 = (s32[8,21]{1,0:T(8,128)S(1)}, s32[8,21]{1,0:T(8,128)}, u32[]{:S(2)}) copy-start(s32[8,21]{1,0:T(8,128)} %param.8) | copy-start | bytes 2020
  83.3 12.1 %copy-start.2 = (s32[8,1]{0,1:T(1,128)S(1)}, s32[8,1]{0,1:T(1,128)}, u32[]{:S(2)}) copy-start(s32[8,1]{0,1:T(1,128)} %param.9) | copy-start | bytes 100
  83.3 307.4 %all-to-all-start = ((bf16[16,128,4096]{1,2,0:T(8,128)(2,1)}), bf16[16,128,4096]{1,2,0:T(8,128)(2,1)}, u32[]{:S(2)}, u32[]{:S(2)}) async-start(bf16[16,128,4096]{1,2,0:T(8,128)(2,1)} %stack.2), calls=%async_computation | async-start | bytes 33554432 | tf_op jit(solution)/shard_map/all_to_all | solution.py:50
  95.2 518.8 %reduce-scatter.2.cloned.1.call-start = ((), (), s32[]{:S(2)}) async-start(), calls=%async_computation.4 | async-start | bytes 12386304 | tf_op jit(solution)/shard_map/reduce_scatter | solution.py:60
Sparse Core Ops, SparseCore 0:
  487.8 126.2 reduce-scatter.1
